TPU v7x, 32 devices: a whole 2x2x4 slice. The times are simulated.
32 devices in a mesh: view: 4 (over z), tile: 8 (over y, x, core).
Axes of the slice: x: 2, y: 2, z: 4, core: 2. Of those that a mesh axis runs over, the one named last changes fastest.
Arguments:
- centres: float32 [3, 32768], P(None, ('view', 'tile')), may hold values from -6 to 6
- shape_raw: float32 [6, 32768], P(None, ('view', 'tile')), may hold values from -1 to 0.2
- opacity_logit: float32 [32768], P(('view', 'tile')), may hold values from -6 to -1
- colours: float32 [3, 32768], P(None, ('view', 'tile')), may hold values from -6 to 6
- camera: float32 [8, 2, 4], replicated, may hold values from -15 to 15
- target: float32 [8, 128, 3, 256], P('view', 'tile'), may hold values from -3 to 3
- intersection_ids: int32 [8, 128, 256], P('view', 'tile'), may hold values from 0 to 32767, as said below
- depth_order: int32 [8, 128, 256], P('view', 'tile'), may hold values from 0 to 255, each once within a row
- live_count: int32 [8, 128], P('view', 'tile'), may hold values from 1 to 256, as said below
Outputs:
- rendered: float32 [8, 128, 3, 256], P('view', 'tile')
- grad_centres: float32 [3, 32768], P(None, ('view', 'tile'))
- grad_shape: float32 [6, 32768], P(None, ('view', 'tile'))
- grad_opacity: float32 [32768], P(('view', 'tile'))
- grad_colours: float32 [3, 32768], P(None, ('view', 'tile'))
- next_owner: int32 [8, 128], P('view', 'tile')
Inputs may be any that keep to these rules, and one draw needn't show every extreme that they name: `intersection_ids`: gaussian g is held by device g div 1024, devices counted along view+tile. Among the 2 x 16 x 256 slots held by one device at most 512 name Gaussians of any one device, and in every draw some device is named exactly 512 times by the slots of every device. `depth_order`: each tile's entries are a permutation of the slot numbers. Slot s of tile (v, t) is live when s < live_count[v, t]; every view has a tile with all 256 slots live.
All inputs are finite; a program needn't handle non-finite values.
Results may differ from a plain program's by a relative error of at most 0.0003.
Values sent between devices are 32-bit elements; how exact they have to be, the bound alone decides.
No kernel may reach another device: no remote copies, remote signals or barrier semaphores. Data moves between devices by JAX's collectives and lax.ppermute only.
A program may use at most 128 MiB of HBM per device.

v0:
```python
from functools import partial
import math
import jax
import jax.numpy as jnp
from jax import lax
from jax.sharding import PartitionSpec as P

SIDE = 16
exact_mode = lax.Precision.HIGHEST


def lower_factor(shape_raw):
    empty_cells = jnp.zeros_like(shape_raw[0])
    first_row = jnp.stack([jnp.exp(shape_raw[0]), empty_cells, empty_cells])
    second_row = jnp.stack([shape_raw[1], jnp.exp(shape_raw[2]), empty_cells])
    third_row = jnp.stack([shape_raw[3], shape_raw[4], jnp.exp(shape_raw[5])])
    return jnp.stack([first_row, second_row, third_row])


def project(centres, shape_raw, opacity_logit, colours, camera):
    view_count = camera.shape[0]
    gaussians = centres.shape[1]
    linear = camera[:, :, 0:3]
    screen = (
        jnp.einsum("vij,jg->vig", linear, centres, precision=exact_mode)
        + camera[:, :, 3][:, :, None]
    )
    factor = jnp.einsum("vik,kjg->vijg", linear, lower_factor(shape_raw), precision=exact_mode)
    var_x = jnp.sum(factor[:, 0] * factor[:, 0], axis=1) + 0.3
    cov_xy = jnp.sum(factor[:, 0] * factor[:, 1], axis=1)
    var_y = jnp.sum(factor[:, 1] * factor[:, 1], axis=1) + 0.3
    determinant = var_x * var_y - cov_xy * cov_xy
    opacity = 0.95 / (1.0 + jnp.exp(-opacity_logit))
    fields = [
        screen[:, 0],
        screen[:, 1],
        var_y / determinant,
        -cov_xy / determinant,
        var_x / determinant,
        jnp.broadcast_to(opacity, (view_count, gaussians)),
    ]
    for channel in range(3):
        fields.append(jnp.broadcast_to(colours[channel], (view_count, gaussians)))
    return jnp.stack(fields)


def pixel_offsets():
    pixel_index = jnp.arange(SIDE * SIDE, dtype=jnp.int32)
    across = (pixel_index % SIDE).astype(jnp.float32) - (SIDE - 1) / 2.0
    downward = (pixel_index // SIDE).astype(jnp.float32) - (SIDE - 1) / 2.0
    return (across, downward)


def render_tile(slot_rec, order, live_count):
    slot_count = order.shape[0]
    picker = (
        order[:, None] == lax.broadcasted_iota(jnp.int32, (slot_count, slot_count), 1)
    ).astype(jnp.float32)
    ordered = jnp.einsum("ks,js->kj", slot_rec, picker, precision=exact_mode)
    active_slots = (order < live_count).astype(jnp.float32)
    across, downward = pixel_offsets()
    delta_x = across[:, None] - ordered[0][None, :]
    delta_y = downward[:, None] - ordered[1][None, :]
    radius = (
        ordered[2] * delta_x * delta_x
        + 2.0 * ordered[3] * delta_x * delta_y
        + ordered[4] * delta_y * delta_y
    )
    coverage = active_slots * ordered[5] * jnp.exp(-0.5 * radius)
    keep_log = jnp.log1p(-coverage)
    earlier = (
        lax.broadcasted_iota(jnp.int32, (slot_count, slot_count), 0)
        < lax.broadcasted_iota(jnp.int32, (slot_count, slot_count), 1)
    ).astype(jnp.float32)
    through = jnp.exp(jnp.dot(keep_log, earlier, precision=exact_mode))
    weights = through * coverage
    return jnp.einsum("ck,pk->cp", ordered[6:9], weights, precision=exact_mode)


def render_block(slot_rec, order, live_count):
    return jax.vmap(render_tile)(slot_rec, order, live_count)


def render_all(slot_rec, order, live_count):
    lead_count, tile_count, slot_count = order.shape
    total_tiles = lead_count * tile_count
    block_size = math.gcd(total_tiles, 8)
    records = jnp.moveaxis(slot_rec, 0, 2).reshape(
        total_tiles // block_size, block_size, 9, slot_count
    )
    orders = order.reshape(total_tiles // block_size, block_size, slot_count)
    counts = live_count.reshape(total_tiles // block_size, block_size)
    blocked = jax.checkpoint(render_block)

    def one_block(packed):
        return blocked(packed[0], packed[1], packed[2])

    images = lax.map(one_block, (records, orders, counts))
    return images.reshape(lead_count, tile_count, 3, SIDE * SIDE)


def slot_ranks(owner_table):
    slots_here, devices = owner_table.shape
    block_rows = math.gcd(slots_here, 512)
    blocks = slots_here // block_rows
    grouped = owner_table.reshape(blocks, block_rows, devices)
    strict = (
        lax.broadcasted_iota(jnp.int32, (block_rows, block_rows), 1)
        < lax.broadcasted_iota(jnp.int32, (block_rows, block_rows), 0)
    ).astype(jnp.float32)
    inner = jnp.einsum("ij,njd->nid", strict, grouped, precision=exact_mode)
    block_totals = jnp.sum(grouped, axis=1)
    block_before = jnp.cumsum(block_totals, axis=0) - block_totals
    ranked = (inner + block_before[:, None, :]) * grouped
    return jnp.sum(ranked, axis=2).reshape(slots_here)


def fetch_rows(flat_rec, wanted):
    return jnp.take(flat_rec, wanted, axis=1)


def return_rows(values, wanted, columns):
    summed = jax.ops.segment_sum(jnp.transpose(values), wanted, num_segments=columns)
    return jnp.transpose(summed)


def shards(
    centres,
    shape_raw,
    opacity_logit,
    colours,
    camera,
    target,
    intersection_ids,
    depth_order,
    live_count,
):
    view_group = lax.axis_size("view")
    tile_group = lax.axis_size("tile")
    devices = view_group * tile_group
    own_count = centres.shape[1]
    views_here, tiles_here, slot_count = intersection_ids.shape
    slots_here = views_here * tiles_here * slot_count
    capacity = 2 * slots_here // devices
    totals = jnp.sum(live_count, axis=1)
    within = jnp.cumsum(live_count, axis=1) - live_count
    table = lax.all_gather(totals[None, :], "tile", axis=0, tiled=True)
    rank_rows = lax.broadcasted_iota(jnp.int32, table.shape, 0)
    before = jnp.sum(jnp.where(rank_rows < lax.axis_index("tile"), table, 0), axis=0)
    whole = jnp.sum(table, axis=0)
    next_owner = (before[:, None] + within) * tile_group // whole[:, None]
    project_here = partial(project, camera=camera)
    records, project_back = jax.vjp(project_here, centres, shape_raw, opacity_logit, colours)
    flat_rec = records.reshape(9, -1)
    rec_columns = flat_rec.shape[1]
    first_view = lax.axis_index("view") * views_here
    view_ids = first_view + lax.broadcasted_iota(jnp.int32, intersection_ids.shape, 0)
    owners = (intersection_ids // own_count).reshape(-1)
    request = (view_ids * own_count + intersection_ids % own_count).reshape(-1).astype(jnp.float32)
    peer_index = lax.broadcasted_iota(jnp.int32, (1, devices), 1)
    owner_table = (owners[:, None] == peer_index).astype(jnp.float32)
    ranks = slot_ranks(owner_table).astype(jnp.int32)
    rank_table = (ranks[:, None] == lax.broadcasted_iota(jnp.int32, (1, capacity), 1)).astype(
        jnp.float32
    )
    send_ids = (
        jnp.einsum("sd,sc->dc", owner_table, request[:, None] * rank_table, precision=exact_mode)
        .astype(jnp.int32)
        .reshape(-1)
    )
    got_ids = lax.all_to_all(send_ids, ("view", "tile"), split_axis=0, concat_axis=0, tiled=True)
    answer = fetch_rows(flat_rec, got_ids)
    fetched = lax.all_to_all(answer, ("view", "tile"), split_axis=1, concat_axis=1, tiled=True)
    by_rank = jnp.einsum(
        "kdc,sc->kds", fetched.reshape(9, devices, capacity), rank_table, precision=exact_mode
    )
    slot_rec = jnp.sum(by_rank * jnp.transpose(owner_table)[None], axis=1).reshape(
        9, views_here, tiles_here, slot_count
    )
    render_here = partial(render_all, order=depth_order, live_count=live_count)
    rendered, pullback = jax.vjp(render_here, slot_rec)
    slot_grad = pullback(rendered - target)[0].reshape(9, -1)
    weighted = slot_grad[:, :, None] * rank_table[None]
    back_buf = jnp.einsum("sd,ksc->kdc", owner_table, weighted, precision=exact_mode).reshape(
        9, devices * capacity
    )
    returned = lax.all_to_all(back_buf, ("view", "tile"), split_axis=1, concat_axis=1, tiled=True)
    record_grad = return_rows(returned, got_ids, rec_columns).reshape(records.shape)
    gradients = project_back(record_grad)
    return (rendered, gradients[0], gradients[1], gradients[2], gradients[3], next_owner)


def solution(mesh):
    in_specs = (
        P(None, ("view", "tile")),
        P(None, ("view", "tile")),
        P(("view", "tile")),
        P(None, ("view", "tile")),
        P(),
        P("view", "tile", None, None),
        P("view", "tile", None),
        P("view", "tile", None),
        P("view", "tile"),
    )
    out_specs = (
        P("view", "tile", None, None),
        P(None, ("view", "tile")),
        P(None, ("view", "tile")),
        P(("view", "tile")),
        P(None, ("view", "tile")),
        P("view", "tile"),
    )
    return jax.shard_map(shards, mesh=mesh, in_specs=in_specs, out_specs=out_specs, check_vma=False)
```

profile of v0, /device:TPU:0, one launch (start us, length us, event | category | flops | bytes accessed | tf_op | source)
XLA Modules:
  0.0 478.5 jit_solution(9977849283200208943)
XLA Ops:
  2.4 7.6 %fusion.128 = s32[32,512,1]{1,0,2:T(8,128)S(1)} fusion(f32[8192]{0:T(1024)S(1)} %bitcast.348, s32[8192]{0:T(1024)S(1)} %bitcast.334, s32[8192]{0:T(1024)S(1)} %bitcast.324), kind=kOutput, calls=%fused_computation.182 | convolution fusion | flops 1619279872 | bytes 163840 | tf_op jit(solution)/shard_map/sd,sc->dc/dot_general | solution.py:167
  10.7 7.3 %all-to-all-start = ((s32[32,512,1]{1,2,0:T(1,128)}), s32[32,512,1]{1,2,0:T(1,128)S(1)}, u32[]{:S(2)}, u32[]{:S(2)}) async-start(s32[32,512,1]{1,2,0:T(1,128)} %copy.67), calls=%async_computation | async-start | bytes 131072 | tf_op jit(solution)/shard_map/all_to_all | solution.py:171
  18.2 6.1 %fusion.103 = f32[8192,512]{1,0:T(8,128)} fusion(s32[8192]{0:T(1024)S(1)} %bitcast.335), kind=kLoop, calls=%fused_computation.155 | loop fusion | flops 8388608 | bytes 16809984 | tf_op jit(solution)/shard_map/convert_element_type | solution.py:163
  29.3 56.6 %gather_fusion = f32[16384,9]{1,0:T(8,128)} fusion(f32[9,8192]{0,1:T(8,128)} %copy.70, s32[16384]{0:T(1024)S(1)} %broadcast_clamp_fusion), kind=kCustom, calls=%fused_computation | custom fusion | bytes 1245184 | tf_op jit(solution)/shard_map/jit(_take)/gather | solution.py:119
  85.9 5.2 %copy.71 = f32[9,32,512]{2,0,1:T(8,128)S(1)} copy(f32[9,32,512]{0,2,1:T(8,128)} %bitcast.307) | data formatting | bytes 1179648 | tf_op jit(solution)/shard_map/jit(_take)/gather | solution.py:119
  92.3 6.0 %all-to-all-start.1 = ((f32[9,32,512]{2,0,1:T(8,128)}), f32[9,32,512]{2,0,1:T(8,128)S(1)}, u32[]{:S(2)}, u32[]{:S(2)}) async-start(f32[9,32,512]{2,0,1:T(8,128)} %broadcast_select_fusion), calls=%async_computation.1 | async-start | bytes 2097152 | tf_op jit(solution)/shard_map/all_to_all | solution.py:173
  98.5 26.0 %all-to-all-done.1 = f32[9,32,512]{2,0,1:T(8,128)S(1)} async-done(((f32[9,32,512]{2,0,1:T(8,128)}), f32[9,32,512]{2,0,1:T(8,128)S(1)}, u32[]{:S(2)}, u32[]{:S(2)}) %all-to-all-start.1) | async-done | bytes 589856 | tf_op jit(solution)/shard_map/all_to_all | solution.py:173
  124.5 13.1 %fusion.114 = f32[9,8192]{1,0:T(8,128)S(1)} fusion(f32[32,8192]{1,0:T(8,128)S(1)} %fusion.135, s32[8192]{0:T(1024)S(1)} %bitcast.336, f32[9,32,512]{2,0,1:T(8,128)S(1)} %all-to-all-done.1), kind=kOutput, calls=%fused_computation.172 | convolution fusion | flops 14504353792 | bytes 1966080 | tf_op jit(solution)/shard_map/kdc,sc->kds/dot_general | solution.py:174
  138.4 30.5 %while.27 = (s32[]{:T(128)}, f32[4,8,3,256]{3,1,0,2:T(8,128)S(1)}, f32[4,8,9,256]{3,2,1,0:T(8,128)S(1)}, s32[4,8,256]{2,1,0:T(8,128)S(1)}, s32[4,8]{1,0:T(4,128)S(1)}, /*index=5*/s32[]{:T(128)}) while((s32[]{:T(128)}, f32[4,8,3,256]{3,1,0,2:T(8,128)S(1)}, f32[4,8,9,256]{3,2,1,0:T(8,128)S(1)}, s32[4,8,256]{2,1,0:T(8,128)S(1)}, ...), condition=%wide.region_8.9_spmd.clone, body=%wide.region_7.8_spmd.clone.sunk | while | flops 1700407296 | bytes 4864185 | solution.py:98
  139.8 3.3 fusion.243
  143.1 2.9 fusion.244
  147.4 3.3 fusion.243
  150.7 2.9 fusion.244
  155.1 3.3 fusion.243
  158.3 2.9 fusion.244
  162.7 3.3 fusion.243
  166.0 2.9 fusion.244
  169.0 62.0 %while.26 = (s32[]{:T(128)}, f32[4,8,9,256]{3,2,1,0:T(8,128)S(1)}, f32[4,8,9,256]{3,2,1,0:T(8,128)S(1)}, s32[4,8,256]{2,1,0:T(8,128)S(1)}, s32[4,8]{1,0:T(4,128)...) while((s32[]{:T(128)}, f32[4,8,9,256]{3,2,1,0:T(8,128)S(1)}, ...), condition=%wide.region_16.17_spmd, body=%wide.region_9.16_spmd.sunk | while | flops 3417032704 | bytes 11907285 | solution.py:98
  177.7 5.9 %fusion.231 = (f32[8,256]{1,0:T(8,128)S(1)}, f32[8,256]{1,0:T(8,128)S(1)}, f32[8,256]{1,0:T(8,128)S(1)}, f32[8,256]{1,0:T(8,128)S(1)}, f32[8,256]{1,0:T(8,128)S(1)}, /*index=5*/f32[8,256]{1,0:T(8,128)S(1)}) fusion(f32[8,256]{1,0:T(8,128)S(1)} %get-tuple-element.492, f32[256]{0:T(256)S(1)} %get-tuple-element.493, ...), kind=kOutput, calls=%fused_computation.30.clone.1 | convolution fusion | flops 1640550400 | bytes 4294656 | tf_op jit(solution)/shard_map/transpose(jvp())/while/body/eval_jaxpr/checkpoint/vmap()/dot_general | solution.py:75
  186.2 2.7 fusion.230
  193.1 5.9 %fusion.231 = (f32[8,256]{1,0:T(8,128)S(1)}, f32[8,256]{1,0:T(8,128)S(1)}, f32[8,256]{1,0:T(8,128)S(1)}, f32[8,256]{1,0:T(8,128)S(1)}, f32[8,256]{1,0:T(8,128)S(1)}, /*index=5*/f32[8,256]{1,0:T(8,128)S(1)}) fusion(f32[8,256]{1,0:T(8,128)S(1)} %get-tuple-element.492, f32[256]{0:T(256)S(1)} %get-tuple-element.493, ...), kind=kOutput, calls=%fused_computation.30.clone.1 | convolution fusion | flops 1640550400 | bytes 4294656 | tf_op jit(solution)/shard_map/transpose(jvp())/while/body/eval_jaxpr/checkpoint/vmap()/dot_general | solution.py:75
  201.6 2.7 fusion.230
  208.5 5.9 %fusion.231 = (f32[8,256]{1,0:T(8,128)S(1)}, f32[8,256]{1,0:T(8,128)S(1)}, f32[8,256]{1,0:T(8,128)S(1)}, f32[8,256]{1,0:T(8,128)S(1)}, f32[8,256]{1,0:T(8,128)S(1)}, /*index=5*/f32[8,256]{1,0:T(8,128)S(1)}) fusion(f32[8,256]{1,0:T(8,128)S(1)} %get-tuple-element.492, f32[256]{0:T(256)S(1)} %get-tuple-element.493, ...), kind=kOutput, calls=%fused_computation.30.clone.1 | convolution fusion | flops 1640550400 | bytes 4294656 | tf_op jit(solution)/shard_map/transpose(jvp())/while/body/eval_jaxpr/checkpoint/vmap()/dot_general | solution.py:75
  217.0 2.7 fusion.230
  224.0 5.9 %fusion.231 = (f32[8,256]{1,0:T(8,128)S(1)}, f32[8,256]{1,0:T(8,128)S(1)}, f32[8,256]{1,0:T(8,128)S(1)}, f32[8,256]{1,0:T(8,128)S(1)}, f32[8,256]{1,0:T(8,128)S(1)}, /*index=5*/f32[8,256]{1,0:T(8,128)S(1)}) fusion(f32[8,256]{1,0:T(8,128)S(1)} %get-tuple-element.492, f32[256]{0:T(256)S(1)} %get-tuple-element.493, ...), kind=kOutput, calls=%fused_computation.30.clone.1 | convolution fusion | flops 1640550400 | bytes 4294656 | tf_op jit(solution)/shard_map/transpose(jvp())/while/body/eval_jaxpr/checkpoint/vmap()/dot_general | solution.py:75
  231.5 68.7 %fusion.121 = f32[9,32,512]{2,1,0:T(8,128)S(1)} fusion(f32[8192,512]{1,0:T(8,128)} %fusion.103, f32[9,8192]{1,0:T(8,128)S(1)} %bitcast.319, pred[8192,32,1]{0,1,2:T(32,128)(4,1)S(1)} %fusion.187), kind=kOutput, calls=%fused_computation.178 | convolution fusion | flops 14533263360 | bytes 17924096 | tf_op jit(solution)/shard_map/sd,ksc->kdc/dot_general | solution.py:184
  301.6 3.6 all-to-all-start.2
  306.8 10.4 %all-reduce.23 = s32[16]{0:T(128)S(1)} all-reduce(s32[16]{0:T(128)S(1)} %dynamic-update-slice), channel_id=2, replica_groups=mesh['view'=4,'tile'=8] {'tile'}, use_global_device_ids=true, to_apply=%add.23 | all-reduce | flops 16 | bytes 128
  319.1 12.4 %all-to-all-done.2 = f32[9,32,512]{2,0,1:T(8,128)S(1)} async-done(((f32[9,32,512]{2,0,1:T(8,128)}), f32[9,32,512]{2,0,1:T(8,128)S(1)}, u32[]{:S(2)}, u32[]{:S(2)}) %all-to-all-start.2) | async-done | bytes 589856 | tf_op jit(solution)/shard_map/all_to_all | solution.py:187
  332.5 4.7 copy.82
  337.2 103.7 %scatter_custom_fusion = f32[8192,9]{1,0:T(8,128)} fusion(s32[16384]{0:T(1024)S(1)} %bitcast.317, f32[16384,9]{1,0:T(8,128)} %copy.82, f32[]{:T(128)} %constant.249.clone.1), kind=kCustom, calls=%fused_computation.173 | custom fusion | flops 147456 | bytes 295424 | tf_op jit(solution)/shard_map/scatter-add | solution.py:123
  440.9 32.8 %slice_reduce_fusion.2 = (f32[8192]{0:T(1024)S(1)}, f32[8192]{0:T(1024)S(1)}, f32[8192]{0:T(1024)S(1)}, f32[8192]{0:T(1024)S(1)}, f32[8192]{0:T(1024)S(1)}, /*in...) fusion(f32[9,8192]{0,1:T(8,128)} %bitcast.306), kind=kLoop, calls=%fused_computation.165 | loop fusion | bytes 589824 | tf_op jit(solution)/shard_map/transpose(jvp())/unstack | solution.py:44
  (264 shorter events, 54.3 us)
Async XLA Ops:
  0.6 24.8 %copy-start = (f32[3,1024]{1,0:T(4,128)S(1)}, f32[3,1024]{1,0:T(4,128)}, u32[]{:S(2)}) copy-start(f32[3,1024]{1,0:T(4,128)} %param.13) | copy-start | bytes 36868
  2.4 15.7 %copy-start.13 = (f32[6,1024]{1,0:T(8,128)S(1)}, f32[6,1024]{1,0:T(8,128)}, u32[]{:S(2)}) copy-start(f32[6,1024]{1,0:T(8,128)} %param.14) | copy-start | bytes 73732
  10.7 18.5 %all-to-all-start = ((s32[32,512,1]{1,2,0:T(1,128)}), s32[32,512,1]{1,2,0:T(1,128)S(1)}, u32[]{:S(2)}, u32[]{:S(2)}) async-start(s32[32,512,1]{1,2,0:T(1,128)} %copy.67), calls=%async_computation | async-start | bytes 131072 | tf_op jit(solution)/shard_map/all_to_all | solution.py:171
  18.2 6.3 %copy-start.11 = (f32[8,2,4]{0,2,1:T(4,128)S(1)}, f32[8,2,4]{0,2,1:T(4,128)}, u32[]{:S(2)}) copy-start(f32[8,2,4]{0,2,1:T(4,128)} %param.17) | copy-start | bytes 772
  18.2 7.0 %copy-start.17 = (f32[3,1024]{1,0:T(4,128)S(1)}, f32[3,1024]{1,0:T(4,128)}, u32[]{:S(2)}) copy-start(f32[3,1024]{1,0:T(4,128)} %param.16) | copy-start | bytes 36868
  18.2 7.6 %copy-start.14 = (f32[1024]{0:T(1024)S(1)}, f32[1024]{0:T(1024)}, u32[]{:S(2)}) copy-start(f32[1024]{0:T(1024)} %param.15) | copy-start | bytes 12292
  24.9 1.0 copy-start.1
  25.0 1.0 copy-start.4
  25.0 1.0 copy-start.6
  25.0 1.0 copy-start.8
  26.4 2.7 copy-start.16
  92.3 32.2 %all-to-all-start.1 = ((f32[9,32,512]{2,0,1:T(8,128)}), f32[9,32,512]{2,0,1:T(8,128)S(1)}, u32[]{:S(2)}, u32[]{:S(2)}) async-start(f32[9,32,512]{2,0,1:T(8,128)} %broadcast_select_fusion), calls=%async_computation.1 | async-start | bytes 2097152 | tf_op jit(solution)/shard_map/all_to_all | solution.py:173
  137.6 0.8 copy-start.3
  138.4 30.5 %copy-start.10 = (f32[2,16,3,256]{3,1,2,0:T(8,128)S(1)}, f32[2,16,3,256]{3,1,2,0:T(8,128)}, u32[]{:S(2)}) copy-start(f32[2,16,3,256]{3,1,2,0:T(8,128)} %param.18) | copy-start | bytes 294916
  300.2 5.1 %copy-start.18 = (u32[32]{0:T(128)S(1)}, u32[32]{0:T(128)}, u32[]{:S(2)}) copy-start(u32[32]{0:T(128)} %constant.321) | copy-start | bytes 388
  301.6 29.8 %all-to-all-start.2 = ((f32[9,32,512]{2,0,1:T(8,128)}), f32[9,32,512]{2,0,1:T(8,128)S(1)}, u32[]{:S(2)}, u32[]{:S(2)}) async-start(f32[9,32,512]{2,0,1:T(8,128)} %copy.80), calls=%async_computation.2 | async-start | bytes 2097152 | tf_op jit(solution)/shard_map/all_to_all | solution.py:187
  440.9 32.9 %copy-start.5 = (f32[8,1024]{1,0:T(8,128)S(1)}, f32[8,1024]{1,0:T(8,128)}, u32[]{:S(2)}) copy-start(f32[8,1024]{1,0:T(8,128)} %copy-done.4) | copy-start | bytes 98308
  440.9 32.9 %copy-start.7 = (f32[8,1024]{1,0:T(8,128)S(1)}, f32[8,1024]{1,0:T(8,128)}, u32[]{:S(2)}) copy-start(f32[8,1024]{1,0:T(8,128)} %copy-done.6) | copy-start | bytes 98308
  440.9 32.9 %copy-start.9 = (f32[8,1024]{1,0:T(8,128)S(1)}, f32[8,1024]{1,0:T(8,128)}, u32[]{:S(2)}) copy-start(f32[8,1024]{1,0:T(8,128)} %copy-done.8) | copy-start | bytes 98308
  440.9 32.9 %copy-start.2 = (f32[8,2,3,1024]{3,0,1,2:T(8,128)S(1)}, f32[8,2,3,1024]{3,0,1,2:T(8,128)}, u32[]{:S(2)}) copy-start(f32[8,2,3,1024]{3,0,1,2:T(8,128)} %copy-done.1) | copy-start | bytes 589828
  440.9 33.0 %copy-start.12 = (f32[8,2,4]{0,2,1:T(4,128)S(1)}, f32[8,2,4]{0,2,1:T(4,128)}, u32[]{:S(2)}) copy-start(f32[8,2,4]{0,2,1:T(4,128)} %param.17) | copy-start | bytes 772
  473.7 1.6 copy-start.15
where the time goes:
time: 487 us; the launch traced here: 479 us
  matrix products  182 us (37%)
  other arithmetic  118 us (24%)
  local copies, waits for them, and re-layouts  110 us (23%)
  waiting for transfers between devices  38.4 us (8%)
  starting transfers between devices  17 us (3%)
  blocking collectives  10.4 us (2%)
    scatter-add x1, other arithmetic, return_rows(): jax.ops.segment_sum(jnp.transpose(values), wanted, num_segments=columns)  104 us
    dot_general x1, matrix products, shards(): jnp.einsum('sd,ksc->kdc', owner_table, weighted, precision=exact_mode)  68.7 us
    gather x2, local copies, waits for them, and re-layouts, fetch_rows(): return jnp.take(flat_rec, wanted, axis=1)  61.8 us
    dot_general x12, matrix products, render_tile(): through = jnp.exp(jnp.dot(keep_log, earlier, precision=exact_mode))  47.6 us
    another operation x10, local copies, waits for them, and re-layouts, project(): return jnp.stack(fields)  35.9 us
    dot_general x12, matrix products, render_tile(): return jnp.einsum('ck,pk->cp', ordered[6:9], weights, precision=exact_mode)  28.1 us
    all_to_all x1, waiting for transfers between devices, shards(): lax.all_to_all(answer, ('view', 'tile'), split_axis=1, concat_axis=1, til...  26 us
    dot_general x12, matrix products, render_tile(): ordered = jnp.einsum('ks,js->kj', slot_rec, picker, precision=exact_mode)  14.3 us
  transfers between devices with their start and end apart: 3, of which 2 were waited for; matrix products, arithmetic and copies ran while one was open for 3% of the time, Pallas kernels for 0%

commit v1 on v0

--- a/solution.py
+++ b/solution.py
@@ -170,7 +170,15 @@
     )
     got_ids = lax.all_to_all(send_ids, ("view", "tile"), split_axis=0, concat_axis=0, tiled=True)
     answer = fetch_rows(flat_rec, got_ids)
-    fetched = lax.all_to_all(answer, ("view", "tile"), split_axis=1, concat_axis=1, tiled=True)
+    fetched = jnp.concatenate(
+        lax.all_to_all(
+            jnp.stack(jnp.split(answer, lax.axis_size(("view", "tile")), axis=1), axis=0),
+            ("view", "tile"),
+            0,
+            0,
+        ),
+        axis=1,
+    )
     by_rank = jnp.einsum(
         "kdc,sc->kds", fetched.reshape(9, devices, capacity), rank_table, precision=exact_mode
     )

time: 487 us -> 520 us (1.068)
  local copies, waits for them, and re-layouts: 110 us -> 134 us
  other arithmetic: 118 us -> 128 us
    unnamed x66 -> x103, local copies, waits for them, and re-layouts: 3.78 us -> 26.3 us
    select_n x2, other arithmetic: 1.22 us -> 11.8 us  [fetch_rows(): return jnp.take(flat_rec, wanted, axis=1)]
    another operation x0 -> x2, local copies, waits for them, and re-layouts: none -> 6.82 us  [shards(): jnp.stack(jnp.split(answer, lax.axis_size(('view', 'tile')), axis=1), axi...]
    gather x2 -> x1, local copies, waits for them, and re-layouts: 61.8 us -> 56.6 us  [fetch_rows(): return jnp.take(flat_rec, wanted, axis=1)]
where the time goes in v1:
time: 520 us; the launch traced here: 513 us
  matrix products  182 us (35%)
  local copies, waits for them, and re-layouts  134 us (26%)
  other arithmetic  128 us (25%)
  waiting for transfers between devices  38.4 us (7%)
  starting transfers between devices  17.1 us (3%)
  blocking collectives  10.4 us (2%)
    scatter-add x1, other arithmetic, return_rows(): jax.ops.segment_sum(jnp.transpose(values), wanted, num_segments=columns)  104 us
    dot_general x1, matrix products, shards(): jnp.einsum('sd,ksc->kdc', owner_table, weighted, precision=exact_mode)  68.9 us
    gather x1, local copies, waits for them, and re-layouts, fetch_rows(): return jnp.take(flat_rec, wanted, axis=1)  56.6 us
    dot_general x12, matrix products, render_tile(): through = jnp.exp(jnp.dot(keep_log, earlier, precision=exact_mode))  47.5 us
    another operation x10, local copies, waits for them, and re-layouts, project(): return jnp.stack(fields)  35.8 us
    dot_general x12, matrix products, render_tile(): return jnp.einsum('ck,pk->cp', ordered[6:9], weights, precision=exact_mode)  28.2 us
    unnamed x103, local copies, waits for them, and re-layouts  26.3 us
    all_to_all x1, waiting for transfers between devices, shards(): lax.all_to_all(jnp.stack(jnp.split(answer, lax.axis_size(('view', 'tile')...  26.1 us
  transfers between devices with their start and end apart: 3, of which 2 were waited for; matrix products, arithmetic and copies ran while one was open for 3% of the time, Pallas kernels for 0%

profile of v1, /device:TPU:0, one launch (start us, length us, event | category | flops | bytes accessed | tf_op | source)
XLA Modules:
  0.0 513.1 jit_solution(14760113837677416998)
XLA Ops:
  2.4 7.6 %fusion.128 = s32[32,512,1]{1,0,2:T(8,128)S(1)} fusion(f32[8192]{0:T(1024)S(1)} %bitcast.474, s32[8192]{0:T(1024)S(1)} %bitcast.460, s32[8192]{0:T(1024)S(1)} %bitcast.450), kind=kOutput, calls=%fused_computation.183 | convolution fusion | flops 1619279872 | bytes 163840 | tf_op jit(solution)/shard_map/sd,sc->dc/dot_general | solution.py:167
  10.7 7.5 %all-to-all-start = ((s32[32,512,1]{1,2,0:T(1,128)}), s32[32,512,1]{1,2,0:T(1,128)S(1)}, u32[]{:S(2)}, u32[]{:S(2)}) async-start(s32[32,512,1]{1,2,0:T(1,128)} %copy.199), calls=%async_computation | async-start | bytes 131072 | tf_op jit(solution)/shard_map/all_to_all | solution.py:171
  18.4 6.1 %fusion.103 = f32[8192,512]{1,0:T(8,128)} fusion(s32[8192]{0:T(1024)S(1)} %bitcast.461), kind=kLoop, calls=%fused_computation.155 | loop fusion | flops 8388608 | bytes 16809984 | tf_op jit(solution)/shard_map/convert_element_type | solution.py:163
  29.5 56.6 %gather_fusion = f32[16384,9]{1,0:T(8,128)} fusion(f32[9,8192]{0,1:T(8,128)} %copy.202, s32[16384]{0:T(1024)S(1)} %broadcast_clamp_fusion), kind=kCustom, calls=%fused_computation | custom fusion | bytes 1245184 | tf_op jit(solution)/shard_map/jit(_take)/gather | solution.py:119
  86.1 11.8 %select_bitcast_fusion.1 = f32[9,16384]{0,1:T(8,128)S(1)} fusion(f32[16384,9]{1,0:T(8,128)} %gather_fusion, pred[16384]{0:T(1024)(128)(4,1)S(1)} %compare_and_fusion), kind=kLoop, calls=%fused_computation.159 | loop fusion | flops 147456 | bytes 1196032 | tf_op jit(solution)/shard_map/jit(_take)/select_n | solution.py:119
  121.1 6.1 %copy.203 = f32[32,9,512]{2,1,0:T(8,128)} copy(f32[32,9,512]{1,2,0:T(8,128)} %fusion.141) | data formatting | bytes 1179648 | tf_op jit(solution)/shard_map/stack | solution.py:175
  127.2 6.0 %all-to-all-start.1 = ((f32[32,9,512]{2,1,0:T(8,128)}), f32[32,9,512]{2,1,0:T(8,128)S(1)}, u32[]{:S(2)}, u32[]{:S(2)}) async-start(f32[32,9,512]{2,1,0:T(8,128)} %copy.203), calls=%async_computation.1 | async-start | bytes 2097152 | tf_op jit(solution)/shard_map/all_to_all | solution.py:174
  133.3 26.1 %all-to-all-done.1 = f32[32,9,512]{2,1,0:T(8,128)S(1)} async-done(((f32[32,9,512]{2,1,0:T(8,128)}), f32[32,9,512]{2,1,0:T(8,128)S(1)}, u32[]{:S(2)}, u32[]{:S(2)}) %all-to-all-start.1) | async-done | bytes 589856 | tf_op jit(solution)/shard_map/all_to_all | solution.py:174
  159.3 13.1 %fusion.114 = f32[9,8192]{1,0:T(8,128)S(1)} fusion(f32[32,8192]{1,0:T(8,128)S(1)} %fusion.135, s32[8192]{0:T(1024)S(1)} %bitcast.462, f32[32,9,512]{2,1,0:T(8,128)S(1)} %all-to-all-done.1), kind=kOutput, calls=%fused_computation.173 | convolution fusion | flops 14504353792 | bytes 1966080 | tf_op jit(solution)/shard_map/kdc,sc->kds/dot_general | solution.py:182
  173.2 30.5 %while.27 = (s32[]{:T(128)}, f32[4,8,3,256]{3,1,0,2:T(8,128)S(1)}, f32[4,8,9,256]{3,2,1,0:T(8,128)S(1)}, s32[4,8,256]{2,1,0:T(8,128)S(1)}, s32[4,8]{1,0:T(4,128)S(1)}, /*index=5*/s32[]{:T(128)}) while((s32[]{:T(128)}, f32[4,8,3,256]{3,1,0,2:T(8,128)S(1)}, f32[4,8,9,256]{3,2,1,0:T(8,128)S(1)}, s32[4,8,256]{2,1,0:T(8,128)S(1)}, ...), condition=%wide.region_8.9_spmd.clone, body=%wide.region_7.8_spmd.clone.sunk | while | flops 1700407296 | bytes 4864185 | solution.py:98
  174.6 3.3 fusion.276
  177.9 2.9 fusion.277
  182.2 3.3 fusion.276
  185.5 2.9 fusion.277
  189.9 3.3 fusion.276
  193.2 2.9 fusion.277
  197.5 3.3 fusion.276
  200.8 2.9 fusion.277
  203.8 61.9 %while.26 = (s32[]{:T(128)}, f32[4,8,9,256]{3,2,1,0:T(8,128)S(1)}, f32[4,8,9,256]{3,2,1,0:T(8,128)S(1)}, s32[4,8,256]{2,1,0:T(8,128)S(1)}, s32[4,8]{1,0:T(4,128)...) while((s32[]{:T(128)}, f32[4,8,9,256]{3,2,1,0:T(8,128)S(1)}, ...), condition=%wide.region_16.17_spmd, body=%wide.region_9.16_spmd.sunk | while | flops 3417032704 | bytes 11907285 | solution.py:98
  205.5 2.7 fusion.263
  212.5 5.9 %fusion.264 = (f32[8,256]{1,0:T(8,128)S(1)}, f32[8,256]{1,0:T(8,128)S(1)}, f32[8,256]{1,0:T(8,128)S(1)}, f32[8,256]{1,0:T(8,128)S(1)}, f32[8,256]{1,0:T(8,128)S(1)}, /*index=5*/f32[8,256]{1,0:T(8,128)S(1)}) fusion(f32[8,256]{1,0:T(8,128)S(1)} %get-tuple-element.526, f32[256]{0:T(256)S(1)} %get-tuple-element.527, ...), kind=kOutput, calls=%fused_computation.30.clone.1 | convolution fusion | flops 1640550400 | bytes 4294656 | tf_op jit(solution)/shard_map/transpose(jvp())/while/body/eval_jaxpr/checkpoint/vmap()/dot_general | solution.py:75
  221.0 2.7 fusion.263
  227.9 5.9 %fusion.264 = (f32[8,256]{1,0:T(8,128)S(1)}, f32[8,256]{1,0:T(8,128)S(1)}, f32[8,256]{1,0:T(8,128)S(1)}, f32[8,256]{1,0:T(8,128)S(1)}, f32[8,256]{1,0:T(8,128)S(1)}, /*index=5*/f32[8,256]{1,0:T(8,128)S(1)}) fusion(f32[8,256]{1,0:T(8,128)S(1)} %get-tuple-element.526, f32[256]{0:T(256)S(1)} %get-tuple-element.527, ...), kind=kOutput, calls=%fused_computation.30.clone.1 | convolution fusion | flops 1640550400 | bytes 4294656 | tf_op jit(solution)/shard_map/transpose(jvp())/while/body/eval_jaxpr/checkpoint/vmap()/dot_general | solution.py:75
  243.3 5.9 %fusion.264 = (f32[8,256]{1,0:T(8,128)S(1)}, f32[8,256]{1,0:T(8,128)S(1)}, f32[8,256]{1,0:T(8,128)S(1)}, f32[8,256]{1,0:T(8,128)S(1)}, f32[8,256]{1,0:T(8,128)S(1)}, /*index=5*/f32[8,256]{1,0:T(8,128)S(1)}) fusion(f32[8,256]{1,0:T(8,128)S(1)} %get-tuple-element.526, f32[256]{0:T(256)S(1)} %get-tuple-element.527, ...), kind=kOutput, calls=%fused_computation.30.clone.1 | convolution fusion | flops 1640550400 | bytes 4294656 | tf_op jit(solution)/shard_map/transpose(jvp())/while/body/eval_jaxpr/checkpoint/vmap()/dot_general | solution.py:75
  258.8 5.9 %fusion.264 = (f32[8,256]{1,0:T(8,128)S(1)}, f32[8,256]{1,0:T(8,128)S(1)}, f32[8,256]{1,0:T(8,128)S(1)}, f32[8,256]{1,0:T(8,128)S(1)}, f32[8,256]{1,0:T(8,128)S(1)}, /*index=5*/f32[8,256]{1,0:T(8,128)S(1)}) fusion(f32[8,256]{1,0:T(8,128)S(1)} %get-tuple-element.526, f32[256]{0:T(256)S(1)} %get-tuple-element.527, ...), kind=kOutput, calls=%fused_computation.30.clone.1 | convolution fusion | flops 1640550400 | bytes 4294656 | tf_op jit(solution)/shard_map/transpose(jvp())/while/body/eval_jaxpr/checkpoint/vmap()/dot_general | solution.py:75
  266.3 68.9 %fusion.121 = f32[9,32,512]{2,1,0:T(8,128)S(1)} fusion(f32[8192,512]{1,0:T(8,128)} %fusion.103, f32[9,8192]{1,0:T(8,128)S(1)} %bitcast.445, pred[8192,32,1]{0,1,2:T(32,128)(4,1)S(1)} %fusion.220), kind=kOutput, calls=%fused_computation.179 | convolution fusion | flops 14533263360 | bytes 17924096 | tf_op jit(solution)/shard_map/sd,ksc->kdc/dot_general | solution.py:192
  336.5 3.6 all-to-all-start.2
  341.8 10.4 %all-reduce.23 = s32[16]{0:T(128)S(1)} all-reduce(s32[16]{0:T(128)S(1)} %dynamic-update-slice), channel_id=2, replica_groups=mesh['view'=4,'tile'=8] {'tile'}, use_global_device_ids=true, to_apply=%add.23 | all-reduce | flops 16 | bytes 128
  354.0 12.4 %all-to-all-done.2 = f32[9,32,512]{2,0,1:T(8,128)S(1)} async-done(((f32[9,32,512]{2,0,1:T(8,128)}), f32[9,32,512]{2,0,1:T(8,128)S(1)}, u32[]{:S(2)}, u32[]{:S(2)}) %all-to-all-start.2) | async-done | bytes 589856 | tf_op jit(solution)/shard_map/all_to_all | solution.py:195
  367.5 4.7 copy.214
  372.1 103.7 %scatter_custom_fusion = f32[8192,9]{1,0:T(8,128)} fusion(s32[16384]{0:T(1024)} %bitcast.443, f32[16384,9]{1,0:T(8,128)} %copy.214, f32[]{:T(128)} %constant.249.clone.1), kind=kCustom, calls=%fused_computation.174 | custom fusion | flops 147456 | bytes 295424 | tf_op jit(solution)/shard_map/scatter-add | solution.py:123
  475.9 32.6 %slice_reduce_fusion.2 = (f32[8192]{0:T(1024)S(1)}, f32[8192]{0:T(1024)S(1)}, f32[8192]{0:T(1024)S(1)}, f32[8192]{0:T(1024)S(1)}, f32[8192]{0:T(1024)S(1)}, /*in...) fusion(f32[9,8192]{0,1:T(8,128)} %bitcast.432), kind=kLoop, calls=%fused_computation.166 | loop fusion | bytes 589824 | tf_op jit(solution)/shard_map/transpose(jvp())/unstack | solution.py:44
  (302 shorter events, 79.1 us)
Async XLA Ops:
  0.6 25.0 %copy-start = (f32[3,1024]{1,0:T(4,128)S(1)}, f32[3,1024]{1,0:T(4,128)}, u32[]{:S(2)}) copy-start(f32[3,1024]{1,0:T(4,128)} %param.13) | copy-start | bytes 36868
  2.4 15.9 %copy-start.15 = (f32[6,1024]{1,0:T(8,128)S(1)}, f32[6,1024]{1,0:T(8,128)}, u32[]{:S(2)}) copy-start(f32[6,1024]{1,0:T(8,128)} %param.14) | copy-start | bytes 73732
  10.7 18.6 %all-to-all-start = ((s32[32,512,1]{1,2,0:T(1,128)}), s32[32,512,1]{1,2,0:T(1,128)S(1)}, u32[]{:S(2)}, u32[]{:S(2)}) async-start(s32[32,512,1]{1,2,0:T(1,128)} %copy.199), calls=%async_computation | async-start | bytes 131072 | tf_op jit(solution)/shard_map/all_to_all | solution.py:171
  18.4 6.3 %copy-start.13 = (f32[8,2,4]{0,2,1:T(4,128)S(1)}, f32[8,2,4]{0,2,1:T(4,128)}, u32[]{:S(2)}) copy-start(f32[8,2,4]{0,2,1:T(4,128)} %param.17) | copy-start | bytes 772
  18.4 7.0 %copy-start.20 = (f32[3,1024]{1,0:T(4,128)S(1)}, f32[3,1024]{1,0:T(4,128)}, u32[]{:S(2)}) copy-start(f32[3,1024]{1,0:T(4,128)} %param.16) | copy-start | bytes 36868
  18.4 7.6 %copy-start.16 = (f32[1024]{0:T(1024)S(1)}, f32[1024]{0:T(1024)}, u32[]{:S(2)}) copy-start(f32[1024]{0:T(1024)} %param.15) | copy-start | bytes 12292
  25.1 1.0 copy-start.2
  25.2 4.1 copy-start.6
  25.2 4.1 copy-start.8
  25.2 4.1 copy-start.10
  26.6 2.7 copy-start.18
  29.4 56.7 %copy-start.4 = (s32[32,512,1]{1,2,0:T(1,128)}, s32[32,512,1]{1,2,0:T(1,128)S(1)}, u32[]{:S(2)}) copy-start(s32[32,512,1]{1,2,0:T(1,128)S(1)} %all-to-all-done) | copy-start | bytes 196612
  127.2 32.2 %all-to-all-start.1 = ((f32[32,9,512]{2,1,0:T(8,128)}), f32[32,9,512]{2,1,0:T(8,128)S(1)}, u32[]{:S(2)}, u32[]{:S(2)}) async-start(f32[32,9,512]{2,1,0:T(8,128)} %copy.203), calls=%async_computation.1 | async-start | bytes 2097152 | tf_op jit(solution)/shard_map/all_to_all | solution.py:174
  172.4 0.8 copy-start.5
  173.2 30.5 %copy-start.12 = (f32[2,16,3,256]{3,1,2,0:T(8,128)S(1)}, f32[2,16,3,256]{3,1,2,0:T(8,128)}, u32[]{:S(2)}) copy-start(f32[2,16,3,256]{3,1,2,0:T(8,128)} %param.18) | copy-start | bytes 294916
  335.2 5.0 copy-start.19
  335.2 5.1 %copy-start.21 = (u32[32]{0:T(128)S(1)}, u32[32]{0:T(128)}, u32[]{:S(2)}) copy-start(u32[32]{0:T(128)} %constant.321) | copy-start | bytes 388
  336.5 29.8 %all-to-all-start.2 = ((f32[9,32,512]{2,0,1:T(8,128)}), f32[9,32,512]{2,0,1:T(8,128)S(1)}, u32[]{:S(2)}, u32[]{:S(2)}) async-start(f32[9,32,512]{2,0,1:T(8,128)} %copy.212), calls=%async_computation.2 | async-start | bytes 2097152 | tf_op jit(solution)/shard_map/all_to_all | solution.py:195
  475.8 32.7 %copy-start.7 = (f32[8,1024]{1,0:T(8,128)S(1)}, f32[8,1024]{1,0:T(8,128)}, u32[]{:S(2)}) copy-start(f32[8,1024]{1,0:T(8,128)} %copy-done.6) | copy-start | bytes 98308
  475.8 32.8 %copy-start.9 = (f32[8,1024]{1,0:T(8,128)S(1)}, f32[8,1024]{1,0:T(8,128)}, u32[]{:S(2)}) copy-start(f32[8,1024]{1,0:T(8,128)} %copy-done.8) | copy-start | bytes 98308
  475.8 32.8 %copy-start.11 = (f32[8,1024]{1,0:T(8,128)S(1)}, f32[8,1024]{1,0:T(8,128)}, u32[]{:S(2)}) copy-start(f32[8,1024]{1,0:T(8,128)} %copy-done.10) | copy-start | bytes 98308
  475.8 32.8 %copy-start.3 = (f32[8,2,3,1024]{3,0,1,2:T(8,128)S(1)}, f32[8,2,3,1024]{3,0,1,2:T(8,128)}, u32[]{:S(2)}) copy-start(f32[8,2,3,1024]{3,0,1,2:T(8,128)} %copy-done.2) | copy-start | bytes 589828
  475.8 32.9 %copy-start.14 = (f32[8,2,4]{0,2,1:T(4,128)S(1)}, f32[8,2,4]{0,2,1:T(4,128)}, u32[]{:S(2)}) copy-start(f32[8,2,4]{0,2,1:T(4,128)} %param.17) | copy-start | bytes 772
  475.9 37.0 %copy-start.1 = (f32[3,1024]{1,0:T(4,128)S(1)}, f32[3,1024]{1,0:T(4,128)}, u32[]{:S(2)}) copy-start(f32[3,1024]{1,0:T(4,128)} %param.13) | copy-start | bytes 36868
  508.5 1.6 copy-start.17
